TPU v7x, 32 devices: a whole 2x2x4 slice. The times are simulated.
32 devices in a mesh: dp: 8 (over z, x), tensor: 4 (over y, core).
Axes of the slice: x: 2, y: 2, z: 4, core: 2. Of those that a mesh axis runs over, the one named last changes fastest.
Arguments:
- patches: bfloat16 [192, 50, 1024], P(('dp', 'tensor')), may hold values from -6 to 6
- keep_index: int32 [192, 50], P(('dp', 'tensor')), may hold values from 0 to 49, each once within a row
- kept_count: int32 [192], P(('dp', 'tensor')), may hold values from 25 to 50, as said below
- norm_gain: float32 [2, 2, 1024], replicated, may hold values from 0.5 to 1.5
- shifts: float32 [2, 4, 1024], replicated, may hold values from -3 to 3
- w_qkv: bfloat16 [2, 1024, 3, 1024], P(None, None, None, 'tensor'), may hold values from -0.1875 to 0.1875
- bias_qv: float32 [2, 2, 1024], P(None, None, 'tensor'), may hold values from -3 to 3
- w_out: bfloat16 [2, 1024, 1024], P(None, 'tensor'), may hold values from -1 to 1
- w_fc1: bfloat16 [2, 1024, 4096], P(None, None, 'tensor'), may hold values from -0.1875 to 0.1875
- bias_fc1: float32 [2, 4096], P(None, 'tensor'), may hold values from -3 to 3
- w_fc2: bfloat16 [2, 4096, 1024], P(None, 'tensor'), may hold values from -0.09375 to 0.09375
- cotangent: bfloat16 [192, 50, 1024], P(('dp', 'tensor')), may hold values from -6 to 6
Outputs:
- layer_out: float32 [192, 50, 1024], P(('dp', 'tensor'))
- grad_patches: float32 [192, 50, 1024], P(('dp', 'tensor'))
- grad_gain: float32 [2, 2, 1024], replicated
- grad_shifts: float32 [2, 4, 1024], replicated
- grad_qkv: float32 [2, 1024, 3, 1024], P(None, 'dp', None, 'tensor')
- grad_bias_qv: float32 [2, 2, 1024], replicated
- grad_out: float32 [2, 1024, 1024], P(None, 'tensor', 'dp')
- grad_fc1: float32 [2, 1024, 4096], P(None, 'dp', 'tensor')
- grad_bias_fc1: float32 [2, 4096], replicated
- grad_fc2: float32 [2, 4096, 1024], P(None, 'tensor', 'dp')
Inputs may be any that keep to these rules, and one draw needn't show every extreme that they name: Each row of keep_index holds every patch index once. `kept_count`: some image keeps all 50 slots and some keeps 25.
All inputs are finite; a program needn't handle non-finite values.
Results may differ from a plain program's by a relative error of at most 0.039.
Values may be sent and summed in bfloat16 or wider, within the bound.
A program may use at most 192 MiB of HBM per device.

v0:
```python
from functools import partial
import jax
import jax.numpy as jnp
from jax import lax
from jax.sharding import PartitionSpec as P

D = 1024
HEAD = 64
FF = 4096
LAYERS = 2
PATCHES = 50
EPS = 1e-06
HIGHEST = lax.Precision.HIGHEST


def norm_rows(values, scaling, offset):
    average = jnp.mean(values, axis=-1, keepdims=True)
    centred = values - average
    variance = jnp.mean(centred * centred, axis=-1, keepdims=True)
    return centred * lax.rsqrt(variance + EPS) * scaling + offset


def spread(rows, counts):
    return (
        lax.all_gather(rows, "tensor", axis=0, tiled=True),
        lax.all_gather(counts, "tensor", axis=0, tiled=True),
    )


def collect(partial_rows):
    return lax.psum_scatter(
        partial_rows.astype(jnp.bfloat16), "tensor", scatter_dimension=0, tiled=True
    ).astype(jnp.float32)


def spread_grad(rows):
    return lax.all_gather(rows, "tensor", axis=0, tiled=True)


def collect_grad(partial_rows):
    return lax.psum_scatter(
        partial_rows.astype(jnp.bfloat16), "tensor", scatter_dimension=0, tiled=True
    ).astype(jnp.float32)


def collect_weight(partial_grad, split_dim):
    return lax.psum_scatter(
        partial_grad.astype(jnp.bfloat16), "dp", scatter_dimension=split_dim, tiled=True
    ).astype(jnp.float32)


def score_block(queries, key_rows, visible, score_scale):
    scores = (
        jnp.einsum("bqhe,bkhe->bhqk", queries, key_rows, preferred_element_type=jnp.float32)
        * score_scale
    )
    return jnp.where(visible[:, None, None, :], scores, -1e30)


def local(
    patches,
    keep_index,
    kept_count,
    norm_gain,
    shifts,
    w_qkv,
    bias_qv,
    w_out,
    w_fc1,
    bias_fc1,
    w_fc2,
    cotangent,
):
    width_local = w_qkv.shape[-1]
    hidden_local = w_fc1.shape[-1]
    heads_local = width_local // HEAD
    score_scale = HEAD ** (-0.5)
    slot_ids = jnp.arange(PATCHES, dtype=jnp.int32)
    selector = (keep_index[:, :, None] == slot_ids[None, None, :]).astype(jnp.bfloat16)
    residual = jnp.einsum("bsp,bpd->bsd", selector, patches, preferred_element_type=jnp.float32)
    stored = []
    visible = None
    shape_heads = None
    image_total = 0
    for layer_no in range(LAYERS):
        normed_own = norm_rows(residual, norm_gain[layer_no, 0], shifts[layer_no, 0]).astype(
            jnp.bfloat16
        )
        normed, counts_all = spread(normed_own, kept_count)
        visible = slot_ids[None, :] < counts_all[:, None]
        image_total = normed.shape[0]
        shape_heads = (image_total, PATCHES, heads_local, HEAD)
        triple = jnp.einsum(
            "bsd,dce->bsce", normed, w_qkv[layer_no], preferred_element_type=jnp.float32
        )
        queries = (triple[:, :, 0] + bias_qv[layer_no, 0]).astype(jnp.bfloat16).reshape(shape_heads)
        key_rows = triple[:, :, 1].astype(jnp.bfloat16).reshape(shape_heads)
        value_rows = (
            (triple[:, :, 2] + bias_qv[layer_no, 1]).astype(jnp.bfloat16).reshape(shape_heads)
        )
        scores = score_block(queries, key_rows, visible, score_scale)
        log_total = jax.nn.logsumexp(scores, axis=-1, keepdims=True)
        attn_weights = jnp.exp(scores - log_total).astype(jnp.bfloat16)
        attended = jnp.einsum(
            "bhqk,bkhe->bqhe", attn_weights, value_rows, preferred_element_type=jnp.float32
        )
        attended = attended.reshape(image_total, PATCHES, width_local).astype(jnp.bfloat16)
        mixed = collect(
            jnp.einsum("bse,ed->bsd", attended, w_out[layer_no], preferred_element_type=jnp.float32)
        )
        middle = residual + mixed + shifts[layer_no, 2]
        normed_mid = norm_rows(middle, norm_gain[layer_no, 1], shifts[layer_no, 1]).astype(
            jnp.bfloat16
        )
        normed_mlp, counts_again = spread(normed_mid, kept_count)
        pre_act = (
            jnp.einsum(
                "bsd,df->bsf", normed_mlp, w_fc1[layer_no], preferred_element_type=jnp.float32
            )
            + bias_fc1[layer_no]
        )
        activated = jax.nn.gelu(pre_act, approximate=False).astype(jnp.bfloat16)
        stored.append(
            (
                residual,
                normed,
                queries,
                key_rows,
                value_rows,
                log_total,
                attended,
                middle,
                normed_mlp,
                pre_act,
                activated,
            )
        )
        mlp_part = collect(
            jnp.einsum(
                "bsf,fd->bsd", activated, w_fc2[layer_no], preferred_element_type=jnp.float32
            )
        )
        residual = middle + mlp_part + shifts[layer_no, 3]
    own_mask = (slot_ids[None, :] < kept_count[:, None]).astype(jnp.float32)[:, :, None]
    layer_out = residual * own_mask
    gradient = cotangent.astype(jnp.float32) * own_mask
    offset_at = lax.axis_index("tensor") * width_local
    hidden_at = lax.axis_index("tensor") * hidden_local
    gain_terms = []
    shift_terms = []
    bias_qv_terms = []
    bias_fc1_terms = []
    weight_terms = []
    for layer_no in reversed(range(LAYERS)):
        (
            residual_in,
            normed,
            queries,
            key_rows,
            value_rows,
            log_total,
            attended,
            middle,
            normed_mlp,
            pre_act,
            activated,
        ) = stored[layer_no]
        grad_mlp = gradient.astype(jnp.bfloat16)
        shift_fc2 = jnp.sum(grad_mlp.astype(jnp.float32), axis=(0, 1))
        grad_rows = spread_grad(grad_mlp)
        d_fc2 = jnp.einsum("bsf,bsd->fd", activated, grad_rows, preferred_element_type=jnp.float32)
        d_act = jnp.einsum(
            "bsd,fd->bsf", grad_rows, w_fc2[layer_no], preferred_element_type=jnp.float32
        )
        gelu_pull = jax.vjp(partial(jax.nn.gelu, approximate=False), pre_act)[1]
        d_pre = gelu_pull(d_act)[0].astype(jnp.bfloat16)
        d_bias_fc1 = jnp.sum(d_pre.astype(jnp.float32), axis=(0, 1))
        d_fc1 = jnp.einsum("bsd,bsf->df", normed_mlp, d_pre, preferred_element_type=jnp.float32)
        d_normed = collect_grad(
            jnp.einsum("bsf,df->bsd", d_pre, w_fc1[layer_no], preferred_element_type=jnp.float32)
        )
        norm_pull = jax.vjp(norm_rows, middle, norm_gain[layer_no, 1], shifts[layer_no, 1])[1]
        d_middle, d_gain_mlp, d_shift_mlp = norm_pull(d_normed)
        gradient = gradient + d_middle
        grad_attn = gradient.astype(jnp.bfloat16)
        shift_attn = jnp.sum(grad_attn.astype(jnp.float32), axis=(0, 1))
        grad_rows = spread_grad(grad_attn)
        d_out = jnp.einsum("bse,bsd->ed", attended, grad_rows, preferred_element_type=jnp.float32)
        d_attended = jnp.einsum(
            "bsd,ed->bse", grad_rows, w_out[layer_no], preferred_element_type=jnp.float32
        )
        d_attended = d_attended.astype(jnp.bfloat16).reshape(shape_heads)
        scores = score_block(queries, key_rows, visible, score_scale)
        probability = jnp.exp(scores - log_total)
        d_values = jnp.einsum(
            "bhqk,bqhe->bkhe",
            probability.astype(jnp.bfloat16),
            d_attended,
            preferred_element_type=jnp.float32,
        )
        d_prob = jnp.einsum(
            "bqhe,bkhe->bhqk", d_attended, value_rows, preferred_element_type=jnp.float32
        )
        centre_term = jnp.sum(probability * d_prob, axis=-1, keepdims=True)
        d_scores = (probability * (d_prob - centre_term)).astype(jnp.bfloat16)
        d_queries = (
            jnp.einsum("bhqk,bkhe->bqhe", d_scores, key_rows, preferred_element_type=jnp.float32)
            * score_scale
        )
        d_keys = (
            jnp.einsum("bhqk,bqhe->bkhe", d_scores, queries, preferred_element_type=jnp.float32)
            * score_scale
        )
        d_triple = jnp.stack([d_queries, d_keys, d_values], axis=2)
        d_triple = d_triple.reshape(image_total, PATCHES, 3, width_local).astype(jnp.bfloat16)
        d_bias_qv = jnp.sum(d_triple[:, :, 0::2].astype(jnp.float32), axis=(0, 1))
        d_qkv = jnp.einsum("bsd,bsce->dce", normed, d_triple, preferred_element_type=jnp.float32)
        d_normed = collect_grad(
            jnp.einsum(
                "bsce,dce->bsd", d_triple, w_qkv[layer_no], preferred_element_type=jnp.float32
            )
        )
        norm_pull = jax.vjp(norm_rows, residual_in, norm_gain[layer_no, 0], shifts[layer_no, 0])[1]
        d_input, d_gain_attn, d_shift_attn = norm_pull(d_normed)
        gradient = gradient + d_input
        gain_terms.insert(0, jnp.stack([d_gain_attn, d_gain_mlp]))
        shift_terms.insert(0, jnp.stack([d_shift_attn, d_shift_mlp, shift_attn, shift_fc2]))
        bias_qv_terms.insert(0, d_bias_qv)
        bias_fc1_terms.insert(0, d_bias_fc1)
        weight_terms.insert(
            0,
            (
                collect_weight(d_qkv, 0),
                collect_weight(d_out, 1),
                collect_weight(d_fc1, 0),
                collect_weight(d_fc2, 1),
            ),
        )
    grad_qkv, grad_out, grad_fc1, grad_fc2 = (
        jnp.stack([entry[k] for entry in weight_terms]) for k in range(4)
    )
    zero_at = offset_at * 0
    qv_full = lax.dynamic_update_slice(
        jnp.zeros((LAYERS, 2, D), jnp.float32),
        jnp.stack(bias_qv_terms),
        (zero_at, zero_at, offset_at),
    )
    fc1_full = lax.dynamic_update_slice(
        jnp.zeros((LAYERS, FF), jnp.float32), jnp.stack(bias_fc1_terms), (zero_at, hidden_at)
    )
    grad_gain, grad_shifts, grad_bias_qv, grad_bias_fc1 = lax.psum(
        (jnp.stack(gain_terms), jnp.stack(shift_terms), qv_full, fc1_full), ("dp", "tensor")
    )
    grad_patches = jnp.einsum(
        "bsp,bsd->bpd", selector.astype(jnp.float32), gradient, precision=HIGHEST
    )
    return (
        layer_out,
        grad_patches,
        grad_gain,
        grad_shifts,
        grad_qkv,
        grad_bias_qv,
        grad_out,
        grad_fc1,
        grad_bias_fc1,
        grad_fc2,
    )


def solution(mesh):
    in_specs = (
        P(("dp", "tensor"), None, None),
        P(("dp", "tensor"), None),
        P(("dp", "tensor")),
        P(),
        P(),
        P(None, None, None, "tensor"),
        P(None, None, "tensor"),
        P(None, "tensor", None),
        P(None, None, "tensor"),
        P(None, "tensor"),
        P(None, "tensor", None),
        P(("dp", "tensor"), None, None),
    )
    out_specs = (
        P(("dp", "tensor"), None, None),
        P(("dp", "tensor"), None, None),
        P(),
        P(),
        P(None, "dp", None, "tensor"),
        P(),
        P(None, "tensor", "dp"),
        P(None, "dp", "tensor"),
        P(),
        P(None, "tensor", "dp"),
    )
    return jax.shard_map(local, mesh=mesh, in_specs=in_specs, out_specs=out_specs, check_vma=False)
```

profile of v0, /device:TPU:8, one launch (start us, length us, event | category | flops | bytes accessed | tf_op | source)
XLA Modules:
  0.0 1404.0 jit_solution(15501463727336067155)
XLA Ops:
  18.6 20.9 %all-gather.9.cloned.1.call-done = bf16[24,50,1024]{2,1,0:T(8,128)(2,1)} async-done(((bf16[6,50,1024]{2,1,0:T(8,128)(2,1)}), bf16[24,50,1024]{2,1,0:T(8,128)(2,1)}) %all-gather.9.cloned.1.call-update) | async-done | bytes 2457616 | tf_op jit(solution)/shard_map/all_gather | solution.py:25
  68.2 35.5 %reduce-scatter.25.cloned.1.call-done = bf16[6,50,1024]{2,1,0:T(8,128)(2,1)} async-done(((bf16[24,50,1024]{2,1,0:T(8,128)(2,1)}), bf16[6,50,1024]{2,1,0:T(8,128)(2,1)}) %reduce-scatter.25.cloned.1.call-update) | async-done | bytes 614416 | tf_op jit(solution)/shard_map/reduce_scatter | solution.py:31
  107.4 25.6 %all-gather.11.cloned.1.call-done = bf16[24,50,1024]{2,1,0:T(8,128)(2,1)} async-done(((bf16[6,50,1024]{2,1,0:T(8,128)(2,1)}), bf16[24,50,1024]{2,1,0:T(8,128)(2,1)}) %all-gather.11.cloned.1.call-update) | async-done | bytes 2457616 | tf_op jit(solution)/shard_map/all_gather | solution.py:25
  140.2 13.3 multiply_convert_fusion.1
  159.5 35.6 %reduce-scatter.27.cloned.1.call-done = bf16[6,50,1024]{2,1,0:T(8,128)(2,1)} async-done(((bf16[24,50,1024]{2,1,0:T(8,128)(2,1)}), bf16[6,50,1024]{2,1,0:T(8,128)(2,1)}) %reduce-scatter.27.cloned.1.call-update) | async-done | bytes 614416 | tf_op jit(solution)/shard_map/reduce_scatter | solution.py:31
  198.3 26.0 %all-gather.13.cloned.1.call-done = bf16[24,50,1024]{2,1,0:T(8,128)(2,1)} async-done(((bf16[6,50,1024]{2,1,0:T(8,128)(2,1)}), bf16[24,50,1024]{2,1,0:T(8,128)(2,1)}) %all-gather.13.cloned.1.call-update) | async-done | bytes 2457616 | tf_op jit(solution)/shard_map/all_gather | solution.py:25
  259.7 35.6 %reduce-scatter.29.cloned.1.call-done = bf16[6,50,1024]{2,1,0:T(8,128)(2,1)} async-done(((bf16[24,50,1024]{2,1,0:T(8,128)(2,1)}), bf16[6,50,1024]{2,1,0:T(8,128)(2,1)}) %reduce-scatter.29.cloned.1.call-update) | async-done | bytes 614416 | tf_op jit(solution)/shard_map/reduce_scatter | solution.py:31
  301.9 23.5 %all-gather.15.cloned.1.call-done = bf16[24,50,1024]{2,1,0:T(8,128)(2,1)} async-done(((bf16[6,50,1024]{2,1,0:T(8,128)(2,1)}), bf16[24,50,1024]{2,1,0:T(8,128)(2,1)}) %all-gather.15.cloned.1.call-update) | async-done | bytes 2457616 | tf_op jit(solution)/shard_map/all_gather | solution.py:25
  334.8 13.5 multiply_convert_fusion
  371.5 35.4 %reduce-scatter.33.cloned.1.call-done = bf16[6,50,1024]{2,1,0:T(8,128)(2,1)} async-done(((bf16[24,50,1024]{2,1,0:T(8,128)(2,1)}), bf16[6,50,1024]{2,1,0:T(8,128)(2,1)}) %reduce-scatter.33.cloned.1.call-update) | async-done | bytes 614416 | tf_op jit(solution)/shard_map/reduce_scatter | solution.py:41
  415.4 26.4 %all-gather.19.cloned.1.call-done = bf16[24,50,1024]{2,1,0:T(8,128)(2,1)} async-done(((bf16[6,50,1024]{2,1,0:T(8,128)(2,1)}), bf16[24,50,1024]{2,1,0:T(8,128)(2,1)}) %all-gather.19.cloned.1.call-update) | async-done | bytes 2457616 | tf_op jit(solution)/shard_map/all_gather | solution.py:37
  491.1 28.5 %reduce-scatter.35.cloned.1.call-done = bf16[6,50,1024]{2,1,0:T(8,128)(2,1)} async-done(((bf16[24,50,1024]{2,1,0:T(8,128)(2,1)}), bf16[6,50,1024]{2,1,0:T(8,128)(2,1)}) %reduce-scatter.35.cloned.1.call-update) | async-done | bytes 614416 | tf_op jit(solution)/shard_map/reduce_scatter | solution.py:41
  524.1 33.6 %reduce-scatter.31.cloned.1.call-done = bf16[6,50,1024]{2,1,0:T(8,128)(2,1)} async-done(((bf16[24,50,1024]{2,1,0:T(8,128)(2,1)}), bf16[6,50,1024]{2,1,0:T(8,128)(2,1)}) %reduce-scatter.31.cloned.1.call-update) | async-done | bytes 614416 | tf_op jit(solution)/shard_map/reduce_scatter | solution.py:31
  562.3 26.4 %all-gather.21.cloned.1.call-done = bf16[24,50,1024]{2,1,0:T(8,128)(2,1)} async-done(((bf16[6,50,1024]{2,1,0:T(8,128)(2,1)}), bf16[24,50,1024]{2,1,0:T(8,128)(2,1)}) %all-gather.21.cloned.1.call-update) | async-done | bytes 2457616 | tf_op jit(solution)/shard_map/all_gather | solution.py:37
  606.5 35.5 %reduce-scatter.37.cloned.1.call-done = bf16[6,50,1024]{2,1,0:T(8,128)(2,1)} async-done(((bf16[24,50,1024]{2,1,0:T(8,128)(2,1)}), bf16[6,50,1024]{2,1,0:T(8,128)(2,1)}) %reduce-scatter.37.cloned.1.call-update) | async-done | bytes 614416 | tf_op jit(solution)/shard_map/reduce_scatter | solution.py:41
  747.5 64.3 %reduce-scatter.51.cloned.1.call-done = bf16[128,256]{1,0:T(8,128)(2,1)} async-done(((bf16[1024,256]{1,0:T(8,128)(2,1)}), bf16[128,256]{1,0:T(8,128)(2,1)}) %reduce-scatter.51.cloned.1.call-update) | async-done | bytes 65552
  812.8 68.6 %reduce-scatter.53.cloned.1.call-done = bf16[128,1024]{1,0:T(8,128)(2,1)} async-done(((bf16[1024,1024]{1,0:T(8,128)(2,1)}), bf16[128,1024]{1,0:T(8,128)(2,1)}) %reduce-scatter.53.cloned.1.call-update) | async-done | bytes 262160
  883.5 68.2 %reduce-scatter.47.cloned.1.call-done = bf16[128,1024]{1,0:T(8,128)(2,1)} async-done(((bf16[1024,1024]{1,0:T(8,128)(2,1)}), bf16[128,1024]{1,0:T(8,128)(2,1)}) %reduce-scatter.47.cloned.1.call-update) | async-done | bytes 262160 | tf_op jit(solution)/shard_map/reduce_scatter | solution.py:47
  951.7 70.2 %reduce-scatter.45.cloned.1.call-done = bf16[128,1024]{1,0:T(8,128)(2,1)} async-done(((bf16[1024,1024]{1,0:T(8,128)(2,1)}), bf16[128,1024]{1,0:T(8,128)(2,1)}) %reduce-scatter.45.cloned.1.call-update) | async-done | bytes 262160 | tf_op jit(solution)/shard_map/reduce_scatter | solution.py:47
  1025.6 61.1 %reduce-scatter.49.cloned.1.call-done = bf16[128,256]{1,0:T(8,128)(2,1)} async-done(((bf16[1024,256]{1,0:T(8,128)(2,1)}), bf16[128,256]{1,0:T(8,128)(2,1)}) %reduce-scatter.49.cloned.1.call-update) | async-done | bytes 65552
  1088.5 66.3 %reduce-scatter.43.cloned.1.call-done = bf16[128,3,256]{2,0,1:T(8,128)(2,1)} async-done(((bf16[1024,3,256]{2,0,1:T(8,128)(2,1)}), bf16[128,3,256]{2,0,1:T(8,128)(2,1)}) %reduce-scatter.43.cloned.1.call-update) | async-done | bytes 196624 | tf_op jit(solution)/shard_map/reduce_scatter | solution.py:47
  1154.8 68.0 %reduce-scatter.41.cloned.1.call-done = bf16[128,3,256]{2,0,1:T(8,128)(2,1)} async-done(((bf16[1024,3,256]{2,0,1:T(8,128)(2,1)}), bf16[128,3,256]{2,0,1:T(8,128)(2,1)}) %reduce-scatter.41.cloned.1.call-update) | async-done | bytes 196624 | tf_op jit(solution)/shard_map/reduce_scatter | solution.py:47
  1224.9 35.4 %reduce-scatter.39.cloned.1.call-done = bf16[6,50,1024]{2,1,0:T(8,128)(2,1)} async-done(((bf16[24,50,1024]{2,1,0:T(8,128)(2,1)}), bf16[6,50,1024]{2,1,0:T(8,128)(2,1)}) %reduce-scatter.39.cloned.1.call-update) | async-done | bytes 614416 | tf_op jit(solution)/shard_map/reduce_scatter | solution.py:41
  1269.8 121.8 %all-reduce.4.cloned.1.call-done = (f32[2,2,1024]{2,1,0:T(2,128)}, f32[2,4,1024]{2,1,0:T(4,128)}, f32[2,2,1024]{2,1,0:T(2,128)}, f32[2,4096]{1,0:T(2,128)}) async-done(((f32[2,2,1024]{2,1,0:T(2,128)}, f32[2,4,1024]{2,1,0:T(4,128)}, f32[2,2,1024]{2,1,0:T(2,128)}, f32[2,4096]{1,0:T(2,128)}), (f32[2,2,1024]{2,1,0:T(2,128)}, f32[2,4,1024]{2,1,0:T(4,128)}, f32[2,2,1024]{2,1,0:T(2,128)}, ...) | async-done | bytes 98320 | tf_op jit(solution)/shard_map/psum | solution.py:251
  (420 shorter events, 348.2 us)
Async XLA Ops:
  11.8 91.9 %reduce-scatter.25.cloned.1.call-start = ((), (), s32[]{:S(2)}) async-start(), calls=%async_computation.17 | async-start | bytes 3440640 | tf_op jit(solution)/shard_map/reduce_scatter | solution.py:31
  68.1 64.9 %all-gather.11.cloned.1.call-start = ((), (), s32[]{:S(2)}) async-start(), calls=%async_computation.18 | async-start | bytes 3440640 | tf_op jit(solution)/shard_map/all_gather | solution.py:25
  106.6 88.5 %reduce-scatter.27.cloned.1.call-start = ((), (), s32[]{:S(2)}) async-start(), calls=%async_computation.19 | async-start | bytes 3440640 | tf_op jit(solution)/shard_map/reduce_scatter | solution.py:31
  159.4 64.9 %all-gather.13.cloned.1.call-start = ((), (), s32[]{:S(2)}) async-start(), calls=%async_computation.20 | async-start | bytes 3440640 | tf_op jit(solution)/shard_map/all_gather | solution.py:25
  197.9 97.4 %reduce-scatter.29.cloned.1.call-start = ((), (), s32[]{:S(2)}) async-start(), calls=%async_computation.21 | async-start | bytes 3440640 | tf_op jit(solution)/shard_map/reduce_scatter | solution.py:31
  259.7 65.7 %all-gather.15.cloned.1.call-start = ((), (), s32[]{:S(2)}) async-start(), calls=%async_computation.22 | async-start | bytes 3440640 | tf_op jit(solution)/shard_map/all_gather | solution.py:25
  298.9 55.0 %all-gather.17.cloned.1.call-start = ((), (), s32[]{:S(2)}) async-start(), calls=%async_computation.24 | async-start | bytes 3440640 | tf_op jit(solution)/shard_map/all_gather | solution.py:37
  301.4 105.6 %reduce-scatter.33.cloned.1.call-start = ((), (), s32[]{:S(2)}) async-start(), calls=%async_computation.25 | async-start | bytes 3440640 | tf_op jit(solution)/shard_map/reduce_scatter | solution.py:41
  371.3 70.5 %all-gather.19.cloned.1.call-start = ((), (), s32[]{:S(2)}) async-start(), calls=%async_computation.26 | async-start | bytes 3440640 | tf_op jit(solution)/shard_map/all_gather | solution.py:37
  415.3 104.3 %reduce-scatter.35.cloned.1.call-start = ((), (), s32[]{:S(2)}) async-start(), calls=%async_computation.27 | async-start | bytes 3440640 | tf_op jit(solution)/shard_map/reduce_scatter | solution.py:41
  484.0 73.7 %reduce-scatter.31.cloned.1.call-start = ((), (), s32[]{:S(2)}) async-start(), calls=%async_computation.23 | async-start | bytes 3440640 | tf_op jit(solution)/shard_map/reduce_scatter | solution.py:31
  491.1 97.6 %all-gather.21.cloned.1.call-start = ((), (), s32[]{:S(2)}) async-start(), calls=%async_computation.28 | async-start | bytes 3440640 | tf_op jit(solution)/shard_map/all_gather | solution.py:37
  562.2 79.8 %reduce-scatter.37.cloned.1.call-start = ((), (), s32[]{:S(2)}) async-start(), calls=%async_computation.29 | async-start | bytes 3440640 | tf_op jit(solution)/shard_map/reduce_scatter | solution.py:41
  606.4 82.7 %all-gather.23.cloned.1.call-start = ((), (), s32[]{:S(2)}) async-start(), calls=%async_computation.30 | async-start | bytes 3440640 | tf_op jit(solution)/shard_map/all_gather | solution.py:37
  648.7 97.4 %reduce-scatter.55.cloned.1.call-start = ((), (), s32[]{:S(2)}) async-start(), calls=%async_computation.39 | async-start | bytes 2359296
  657.4 154.3 %reduce-scatter.51.cloned.1.call-start = ((), (), s32[]{:S(2)}) async-start(), calls=%async_computation.37 | async-start | bytes 589824
  664.2 217.2 %reduce-scatter.53.cloned.1.call-start = ((), (), s32[]{:S(2)}) async-start(), calls=%async_computation.38 | async-start | bytes 2359296
  674.7 277.0 %reduce-scatter.47.cloned.1.call-start = ((), (), s32[]{:S(2)}) async-start(), calls=%async_computation.35 | async-start | bytes 2359296 | tf_op jit(solution)/shard_map/reduce_scatter | solution.py:47
  682.5 339.5 %reduce-scatter.45.cloned.1.call-start = ((), (), s32[]{:S(2)}) async-start(), calls=%async_computation.34 | async-start | bytes 2359296 | tf_op jit(solution)/shard_map/reduce_scatter | solution.py:47
  689.1 397.7 %reduce-scatter.49.cloned.1.call-start = ((), (), s32[]{:S(2)}) async-start(), calls=%async_computation.36 | async-start | bytes 589824
  694.0 460.8 %reduce-scatter.43.cloned.1.call-start = ((), (), s32[]{:S(2)}) async-start(), calls=%async_computation.33 | async-start | bytes 1769472 | tf_op jit(solution)/shard_map/reduce_scatter | solution.py:47
  699.7 523.1 %reduce-scatter.41.cloned.1.call-start = ((), (), s32[]{:S(2)}) async-start(), calls=%async_computation.32 | async-start | bytes 1769472 | tf_op jit(solution)/shard_map/reduce_scatter | solution.py:47
  730.7 529.6 %reduce-scatter.39.cloned.1.call-start = ((), (), s32[]{:S(2)}) async-start(), calls=%async_computation.31 | async-start | bytes 3440640 | tf_op jit(solution)/shard_map/reduce_scatter | solution.py:41
  737.2 654.4 %all-reduce.4.cloned.1.call-start = ((), (), s32[]{:S(2)}) async-start(), calls=%async_computation.40 | async-start | bytes 196608 | tf_op jit(solution)/shard_map/psum | solution.py:251
  (101 other events, 6898.8 us)
Sparse Core Ops, SparseCore 0:
  12.0 27.4 all-gather.8
  68.3 35.4 reduce-scatter.24
  106.7 26.2 all-gather.10
  159.6 35.4 reduce-scatter.26
  198.0 26.2 all-gather.12
  259.8 35.4 reduce-scatter.28
  299.0 26.2 all-gather.14
  327.6 26.2 all-gather.16
  371.4 35.4 reduce-scatter.32
  415.4 26.3 all-gather.18
  484.1 35.4 reduce-scatter.34
  522.2 35.4 reduce-scatter.30
  606.5 35.4 reduce-scatter.36
  648.8 26.3 all-gather.22
  678.9 67.1 reduce-scatter.54
  750.2 61.4 reduce-scatter.50
  815.1 66.1 reduce-scatter.52
  884.9 66.7 reduce-scatter.46
  955.1 66.8 reduce-scatter.44
  1025.3 61.4 reduce-scatter.48
  1090.6 64.1 reduce-scatter.42
  1158.3 64.4 reduce-scatter.40
  1225.4 34.8 reduce-scatter.38
  1267.6 123.9 all-reduce.3
  (1 shorter events, 26.2 us)
where the time goes:
time: 1420 us; the launch traced here: 1400 us
  waiting for transfers between devices  1030 us (73%)
  matrix products  164 us (12%)
  local copies, waits for them, and re-layouts  99.5 us (7%)
  other arithmetic  89.3 us (6%)
  between operations  16.6 us (1%)
    reduce_scatter x4, waiting for transfers between devices, collect_weight(): lax.psum_scatter(partial_grad.astype(jnp.bfloat16), 'dp', scatter_dimensi...  273 us
    unnamed x29, waiting for transfers between devices  203 us
    reduce_scatter x4, waiting for transfers between devices, collect(): lax.psum_scatter(partial_rows.astype(jnp.bfloat16), 'tensor', scatter_dim...  140 us
    reduce_scatter x4, waiting for transfers between devices, collect_grad(): lax.psum_scatter(partial_rows.astype(jnp.bfloat16), 'tensor', scatter_dim...  135 us
    psum x1, waiting for transfers between devices, local(): lax.psum((jnp.stack(gain_terms), jnp.stack(shift_terms), qv_full, fc1_ful...  122 us
    all_gather x4, waiting for transfers between devices, spread(): lax.all_gather(rows, 'tensor', axis=0, tiled=True)  96 us
    all_gather x4, waiting for transfers between devices, spread_grad(): return lax.all_gather(rows, 'tensor', axis=0, tiled=True)  58.4 us
    unnamed x219, local copies, waits for them, and re-layouts  41.5 us
  transfers between devices with their start and end apart: 25, of which 24 were waited for; matrix products, arithmetic and copies ran while one was open for 10% of the time, Pallas kernels for 0%

commit v1 on v0

--- a/solution.py
+++ b/solution.py
@@ -13,6 +13,27 @@
 HIGHEST = lax.Precision.HIGHEST
 
 
+def laid_out(blocks, dim):
+    lengths = list(blocks.shape[1:])
+    lengths[dim] *= blocks.shape[0]
+    return jnp.moveaxis(blocks, 0, dim).reshape(lengths)
+
+
+def doubled(array, axis):
+    devices, index = (lax.axis_size(axis), lax.axis_index(axis))
+    pieces, distance = (array[None], 1)
+    while distance < devices:
+        other = lax.ppermute(pieces, axis, [(i, i ^ distance) for i in range(devices)])
+        low = index & distance == 0
+        pieces = jnp.concatenate([jnp.where(low, pieces, other), jnp.where(low, other, pieces)])
+        distance *= 2
+    return pieces
+
+
+def doubled_up(x, axis, dim):
+    return laid_out(doubled(x, axis), dim)
+
+
 def norm_rows(values, scaling, offset):
     average = jnp.mean(values, axis=-1, keepdims=True)
     centred = values - average
@@ -34,7 +55,7 @@
 
 
 def spread_grad(rows):
-    return lax.all_gather(rows, "tensor", axis=0, tiled=True)
+    return doubled_up(rows, "tensor", 0)
 
 
 def collect_grad(partial_rows):

time: 1420 us -> 1400 us (0.986)
    ppermute x0 -> x8, waiting for transfers between devices: none -> 136 us  [doubled(): lax.ppermute(pieces, axis, [(i, i ^ distance) for i in range(devices)])]
    all_gather x4 -> x0, waiting for transfers between devices: 58.4 us -> none  [spread_grad(): return lax.all_gather(rows, 'tensor', axis=0, tiled=True)]
    reduce_scatter x4, waiting for transfers between devices: 135 us -> 99.6 us  [collect_grad(): lax.psum_scatter(partial_rows.astype(jnp.bfloat16), 'tensor', scatter_dim...]
    unnamed x29 -> x25, waiting for transfers between devices: 203 us -> 170 us
    all_gather x4, waiting for transfers between devices: 96 us -> 73.1 us  [spread(): lax.all_gather(rows, 'tensor', axis=0, tiled=True)]
    unnamed x219 -> x237, local copies, waits for them, and re-layouts: 41.5 us -> 48.6 us
  transfers between devices with their start and end apart: 25 -> 29, of which waited for: 24 -> 26; matrix products, arithmetic and copies ran while one was open for 10% -> 9% of each run, Pallas kernels for 0% -> 0%
where the time goes in v1:
time: 1400 us; the launch traced here: 1390 us
  waiting for transfers between devices  1020 us (73%)
  matrix products  150 us (11%)
  local copies, waits for them, and re-layouts  109 us (8%)
  other arithmetic  86.3 us (6%)
  between operations  16.9 us (1%)
    reduce_scatter x4, waiting for transfers between devices, collect_weight(): lax.psum_scatter(partial_grad.astype(jnp.bfloat16), 'dp', scatter_dimensi...  272 us
    unnamed x25, waiting for transfers between devices  170 us
    reduce_scatter x4, waiting for transfers between devices, collect(): lax.psum_scatter(partial_rows.astype(jnp.bfloat16), 'tensor', scatter_dim...  141 us
    ppermute x8, waiting for transfers between devices, doubled(): lax.ppermute(pieces, axis, [(i, i ^ distance) for i in range(devices)])  136 us
    psum x1, waiting for transfers between devices, local(): lax.psum((jnp.stack(gain_terms), jnp.stack(shift_terms), qv_full, fc1_ful...  124 us
    reduce_scatter x4, waiting for transfers between devices, collect_grad(): lax.psum_scatter(partial_rows.astype(jnp.bfloat16), 'tensor', scatter_dim...  99.6 us
    all_gather x4, waiting for transfers between devices, spread(): lax.all_gather(rows, 'tensor', axis=0, tiled=True)  73.1 us
    unnamed x237, local copies, waits for them, and re-layouts  48.6 us
  transfers between devices with their start and end apart: 29, of which 26 were waited for; matrix products, arithmetic and copies ran while one was open for 9% of the time, Pallas kernels for 0%

profile of v1, /device:TPU:8, one launch (start us, length us, event | category | flops | bytes accessed | tf_op | source)
XLA Modules:
  0.0 1387.9 jit_solution(784194232037386536)
XLA Ops:
  18.5 20.9 %all-gather.5.cloned.1.call-done = bf16[24,50,1024]{2,1,0:T(8,128)(2,1)} async-done(((bf16[6,50,1024]{2,1,0:T(8,128)(2,1)}), bf16[24,50,1024]{2,1,0:T(8,128)(2,1)}) %all-gather.5.cloned.1.call-update) | async-done | bytes 2457616 | tf_op jit(solution)/shard_map/all_gather | solution.py:46
  68.3 35.6 %reduce-scatter.25.cloned.1.call-done = bf16[6,50,1024]{2,1,0:T(8,128)(2,1)} async-done(((bf16[24,50,1024]{2,1,0:T(8,128)(2,1)}), bf16[6,50,1024]{2,1,0:T(8,128)(2,1)}) %reduce-scatter.25.cloned.1.call-update) | async-done | bytes 614416 | tf_op jit(solution)/shard_map/reduce_scatter | solution.py:52
  107.0 26.2 %all-gather.7.cloned.1.call-done = bf16[24,50,1024]{2,1,0:T(8,128)(2,1)} async-done(((bf16[6,50,1024]{2,1,0:T(8,128)(2,1)}), bf16[24,50,1024]{2,1,0:T(8,128)(2,1)}) %all-gather.7.cloned.1.call-update) | async-done | bytes 2457616 | tf_op jit(solution)/shard_map/all_gather | solution.py:46
  140.3 13.4 multiply_convert_fusion.1
  159.7 35.6 %reduce-scatter.27.cloned.1.call-done = bf16[6,50,1024]{2,1,0:T(8,128)(2,1)} async-done(((bf16[24,50,1024]{2,1,0:T(8,128)(2,1)}), bf16[6,50,1024]{2,1,0:T(8,128)(2,1)}) %reduce-scatter.27.cloned.1.call-update) | async-done | bytes 614416 | tf_op jit(solution)/shard_map/reduce_scatter | solution.py:52
  198.6 26.0 %all-gather.9.cloned.1.call-done = bf16[24,50,1024]{2,1,0:T(8,128)(2,1)} async-done(((bf16[6,50,1024]{2,1,0:T(8,128)(2,1)}), bf16[24,50,1024]{2,1,0:T(8,128)(2,1)}) %all-gather.9.cloned.1.call-update) | async-done | bytes 2457616 | tf_op jit(solution)/shard_map/all_gather | solution.py:46
  253.3 35.6 %reduce-scatter.29.cloned.1.call-done = bf16[6,50,1024]{2,1,0:T(8,128)(2,1)} async-done(((bf16[24,50,1024]{2,1,0:T(8,128)(2,1)}), bf16[6,50,1024]{2,1,0:T(8,128)(2,1)}) %reduce-scatter.29.cloned.1.call-update) | async-done | bytes 614416 | tf_op jit(solution)/shard_map/reduce_scatter | solution.py:52
  301.6 41.4 %collective-permute-done.1 = bf16[2,6,50,1024]{3,0,2,1:T(2,128)(2,1)} collective-permute-done((bf16[2,6,50,1024]{3,0,2,1:T(2,128)(2,1)}, bf16[2,6,50,1024]{3,0,2,1:T(2,128)(2,1)}, u32[]{:S(2)}, u32[]{:S(2)}) %collective-permute-start.1) | collective-permute-done | bytes 1228832 | tf_op jit(solution)/shard_map/ppermute | solution.py:26
  353.9 13.4 multiply_convert_fusion
  380.7 35.5 %reduce-scatter.33.cloned.1.call-done = bf16[6,50,1024]{2,1,0:T(8,128)(2,1)} async-done(((bf16[24,50,1024]{2,1,0:T(8,128)(2,1)}), bf16[6,50,1024]{2,1,0:T(8,128)(2,1)}) %reduce-scatter.33.cloned.1.call-update) | async-done | bytes 614416 | tf_op jit(solution)/shard_map/reduce_scatter | solution.py:62
  426.2 28.5 %collective-permute-done.3 = bf16[2,6,50,1024]{3,0,2,1:T(2,128)(2,1)S(1)} collective-permute-done((bf16[2,6,50,1024]{3,0,2,1:T(2,128)(2,1)S(1)}, bf16[2,6,50,1024]{3,0,2,1:T(2,128)(2,1)S(1)}, u32[]{:S(2)}, u32[]{:S(2)}) %collective-permute-start.3) | collective-permute-done | bytes 1228832 | tf_op jit(solution)/shard_map/ppermute | solution.py:26
  504.7 28.6 %reduce-scatter.35.cloned.1.call-done = bf16[6,50,1024]{2,1,0:T(8,128)(2,1)} async-done(((bf16[24,50,1024]{2,1,0:T(8,128)(2,1)}), bf16[6,50,1024]{2,1,0:T(8,128)(2,1)}) %reduce-scatter.35.cloned.1.call-update) | async-done | bytes 614416 | tf_op jit(solution)/shard_map/reduce_scatter | solution.py:62
  536.7 34.7 %reduce-scatter.31.cloned.1.call-done = bf16[6,50,1024]{2,1,0:T(8,128)(2,1)} async-done(((bf16[24,50,1024]{2,1,0:T(8,128)(2,1)}), bf16[6,50,1024]{2,1,0:T(8,128)(2,1)}) %reduce-scatter.31.cloned.1.call-update) | async-done | bytes 614416 | tf_op jit(solution)/shard_map/reduce_scatter | solution.py:52
  580.0 28.5 %collective-permute-done.5 = bf16[2,6,50,1024]{3,0,2,1:T(2,128)(2,1)S(1)} collective-permute-done((bf16[2,6,50,1024]{3,0,2,1:T(2,128)(2,1)S(1)}, bf16[2,6,50,1024]{3,0,2,1:T(2,128)(2,1)S(1)}, u32[]{:S(2)}, u32[]{:S(2)}) %collective-permute-start.5) | collective-permute-done | bytes 1228832 | tf_op jit(solution)/shard_map/ppermute | solution.py:26
  677.4 28.6 %collective-permute-done.7 = bf16[2,6,50,1024]{3,0,2,1:T(2,128)(2,1)S(1)} collective-permute-done((bf16[2,6,50,1024]{3,0,2,1:T(2,128)(2,1)S(1)}, bf16[2,6,50,1024]{3,0,2,1:T(2,128)(2,1)S(1)}, u32[]{:S(2)}, u32[]{:S(2)}) %collective-permute-start.7) | collective-permute-done | bytes 1228832 | tf_op jit(solution)/shard_map/ppermute | solution.py:26
  755.9 40.7 %reduce-scatter.51.cloned.1.call-done = bf16[128,256]{1,0:T(8,128)(2,1)} async-done(((bf16[1024,256]{1,0:T(8,128)(2,1)}), bf16[128,256]{1,0:T(8,128)(2,1)}) %reduce-scatter.51.cloned.1.call-update) | async-done | bytes 65552
  797.6 68.3 %reduce-scatter.53.cloned.1.call-done = bf16[128,1024]{1,0:T(8,128)(2,1)} async-done(((bf16[1024,1024]{1,0:T(8,128)(2,1)}), bf16[128,1024]{1,0:T(8,128)(2,1)}) %reduce-scatter.53.cloned.1.call-update) | async-done | bytes 262160
  868.1 67.9 %reduce-scatter.47.cloned.1.call-done = bf16[128,1024]{1,0:T(8,128)(2,1)} async-done(((bf16[1024,1024]{1,0:T(8,128)(2,1)}), bf16[128,1024]{1,0:T(8,128)(2,1)}) %reduce-scatter.47.cloned.1.call-update) | async-done | bytes 262160 | tf_op jit(solution)/shard_map/reduce_scatter | solution.py:68
  936.0 70.1 %reduce-scatter.45.cloned.1.call-done = bf16[128,1024]{1,0:T(8,128)(2,1)} async-done(((bf16[1024,1024]{1,0:T(8,128)(2,1)}), bf16[128,1024]{1,0:T(8,128)(2,1)}) %reduce-scatter.45.cloned.1.call-update) | async-done | bytes 262160 | tf_op jit(solution)/shard_map/reduce_scatter | solution.py:68
  1009.8 61.1 %reduce-scatter.49.cloned.1.call-done = bf16[128,256]{1,0:T(8,128)(2,1)} async-done(((bf16[1024,256]{1,0:T(8,128)(2,1)}), bf16[128,256]{1,0:T(8,128)(2,1)}) %reduce-scatter.49.cloned.1.call-update) | async-done | bytes 65552
  1072.6 66.2 %reduce-scatter.43.cloned.1.call-done = bf16[128,3,256]{2,0,1:T(8,128)(2,1)} async-done(((bf16[1024,3,256]{2,0,1:T(8,128)(2,1)}), bf16[128,3,256]{2,0,1:T(8,128)(2,1)}) %reduce-scatter.43.cloned.1.call-update) | async-done | bytes 196624 | tf_op jit(solution)/shard_map/reduce_scatter | solution.py:68
  1138.8 67.9 %reduce-scatter.41.cloned.1.call-done = bf16[128,3,256]{2,0,1:T(8,128)(2,1)} async-done(((bf16[1024,3,256]{2,0,1:T(8,128)(2,1)}), bf16[128,3,256]{2,0,1:T(8,128)(2,1)}) %reduce-scatter.41.cloned.1.call-update) | async-done | bytes 196624 | tf_op jit(solution)/shard_map/reduce_scatter | solution.py:68
  1208.7 35.5 %reduce-scatter.39.cloned.1.call-done = bf16[6,50,1024]{2,1,0:T(8,128)(2,1)} async-done(((bf16[24,50,1024]{2,1,0:T(8,128)(2,1)}), bf16[6,50,1024]{2,1,0:T(8,128)(2,1)}) %reduce-scatter.39.cloned.1.call-update) | async-done | bytes 614416 | tf_op jit(solution)/shard_map/reduce_scatter | solution.py:62
  1251.5 124.0 %all-reduce.4.cloned.1.call-done = (f32[2,2,1024]{2,1,0:T(2,128)}, f32[2,4,1024]{2,1,0:T(4,128)}, f32[2,2,1024]{2,1,0:T(2,128)}, f32[2,4096]{1,0:T(2,128)}) async-done(((f32[2,2,1024]{2,1,0:T(2,128)}, f32[2,4,1024]{2,1,0:T(4,128)}, f32[2,2,1024]{2,1,0:T(2,128)}, f32[2,4096]{1,0:T(2,128)}), (f32[2,2,1024]{2,1,0:T(2,128)}, f32[2,4,1024]{2,1,0:T(4,128)}, f32[2,2,1024]{2,1,0:T(2,128)}, ...) | async-done | bytes 98320 | tf_op jit(solution)/shard_map/psum | solution.py:272
  (466 shorter events, 337.0 us)
Async XLA Ops:
  7.2 32.1 %all-gather.5.cloned.1.call-start = ((), (), s32[]{:S(2)}) async-start(), calls=%async_computation.16 | async-start | bytes 3440640 | tf_op jit(solution)/shard_map/all_gather | solution.py:46
  11.7 92.2 %reduce-scatter.25.cloned.1.call-start = ((), (), s32[]{:S(2)}) async-start(), calls=%async_computation.17 | async-start | bytes 3440640 | tf_op jit(solution)/shard_map/reduce_scatter | solution.py:52
  68.2 65.0 %all-gather.7.cloned.1.call-start = ((), (), s32[]{:S(2)}) async-start(), calls=%async_computation.18 | async-start | bytes 3440640 | tf_op jit(solution)/shard_map/all_gather | solution.py:46
  106.7 88.5 %reduce-scatter.27.cloned.1.call-start = ((), (), s32[]{:S(2)}) async-start(), calls=%async_computation.19 | async-start | bytes 3440640 | tf_op jit(solution)/shard_map/reduce_scatter | solution.py:52
  159.7 64.9 %all-gather.9.cloned.1.call-start = ((), (), s32[]{:S(2)}) async-start(), calls=%async_computation.20 | async-start | bytes 3440640 | tf_op jit(solution)/shard_map/all_gather | solution.py:46
  198.1 90.7 %reduce-scatter.29.cloned.1.call-start = ((), (), s32[]{:S(2)}) async-start(), calls=%async_computation.21 | async-start | bytes 3440640 | tf_op jit(solution)/shard_map/reduce_scatter | solution.py:52
  253.2 93.6 %all-gather.11.cloned.1.call-start = ((), (), s32[]{:S(2)}) async-start(), calls=%async_computation.22 | async-start | bytes 3440640 | tf_op jit(solution)/shard_map/all_gather | solution.py:46
  291.7 124.5 %reduce-scatter.33.cloned.1.call-start = ((), (), s32[]{:S(2)}) async-start(), calls=%async_computation.24 | async-start | bytes 3440640 | tf_op jit(solution)/shard_map/reduce_scatter | solution.py:62
  301.0 42.0 %collective-permute-start.1 = (bf16[2,6,50,1024]{3,0,2,1:T(2,128)(2,1)}, bf16[2,6,50,1024]{3,0,2,1:T(2,128)(2,1)}, u32[]{:S(2)}, u32[]{:S(2)}) collective-permute-start(bf16[2,6,50,1024]{3,0,2,1:T(2,128)(2,1)} %copy.109), channel_id=1, source_target_pairs={{0,2},{1,3},{2,0},{3,1},{4,6},{5,7},{6,4},{7,5},{8,10},{9,11},{10,... | collective-permute-start | bytes 3686408 | tf_op jit(solution)/shard_map/ppermute | solution.py:26
  380.6 152.7 %reduce-scatter.35.cloned.1.call-start = ((), (), s32[]{:S(2)}) async-start(), calls=%async_computation.25 | async-start | bytes 3440640 | tf_op jit(solution)/shard_map/reduce_scatter | solution.py:62
  425.6 29.1 %collective-permute-start.3 = (bf16[2,6,50,1024]{3,0,2,1:T(2,128)(2,1)S(1)}, bf16[2,6,50,1024]{3,0,2,1:T(2,128)(2,1)S(1)}, u32[]{:S(2)}, u32[]{:S(2)}) collective-permute-start(bf16[2,6,50,1024]{3,0,2,1:T(2,128)(2,1)S(1)} %copy.112), channel_id=1, source_target_pairs={{0,2},{1,3},{2,0},{3,1},{4,6},{5,7},{6,4},{7,5},{8,10},{9,11},{10,... | collective-permute-start | bytes 3686408 | tf_op jit(solution)/shard_map/ppermute | solution.py:26
  497.6 73.7 %reduce-scatter.31.cloned.1.call-start = ((), (), s32[]{:S(2)}) async-start(), calls=%async_computation.23 | async-start | bytes 3440640 | tf_op jit(solution)/shard_map/reduce_scatter | solution.py:52
  504.7 164.1 %reduce-scatter.37.cloned.1.call-start = ((), (), s32[]{:S(2)}) async-start(), calls=%async_computation.26 | async-start | bytes 3440640 | tf_op jit(solution)/shard_map/reduce_scatter | solution.py:62
  579.4 29.1 %collective-permute-start.5 = (bf16[2,6,50,1024]{3,0,2,1:T(2,128)(2,1)S(1)}, bf16[2,6,50,1024]{3,0,2,1:T(2,128)(2,1)S(1)}, u32[]{:S(2)}, u32[]{:S(2)}) collective-permute-start(bf16[2,6,50,1024]{3,0,2,1:T(2,128)(2,1)S(1)} %copy.128), channel_id=1, source_target_pairs={{0,2},{1,3},{2,0},{3,1},{4,6},{5,7},{6,4},{7,5},{8,10},{9,11},{10,... | collective-permute-start | bytes 3686408 | tf_op jit(solution)/shard_map/ppermute | solution.py:26
  624.3 129.8 %reduce-scatter.55.cloned.1.call-start = ((), (), s32[]{:S(2)}) async-start(), calls=%async_computation.35 | async-start | bytes 2359296
  636.8 159.8 %reduce-scatter.51.cloned.1.call-start = ((), (), s32[]{:S(2)}) async-start(), calls=%async_computation.33 | async-start | bytes 589824
  643.6 222.4 %reduce-scatter.53.cloned.1.call-start = ((), (), s32[]{:S(2)}) async-start(), calls=%async_computation.34 | async-start | bytes 2359296
  654.4 281.6 %reduce-scatter.47.cloned.1.call-start = ((), (), s32[]{:S(2)}) async-start(), calls=%async_computation.31 | async-start | bytes 2359296 | tf_op jit(solution)/shard_map/reduce_scatter | solution.py:68
  662.2 343.9 %reduce-scatter.45.cloned.1.call-start = ((), (), s32[]{:S(2)}) async-start(), calls=%async_computation.30 | async-start | bytes 2359296 | tf_op jit(solution)/shard_map/reduce_scatter | solution.py:68
  668.8 402.1 %reduce-scatter.49.cloned.1.call-start = ((), (), s32[]{:S(2)}) async-start(), calls=%async_computation.32 | async-start | bytes 589824
  711.2 427.6 %reduce-scatter.43.cloned.1.call-start = ((), (), s32[]{:S(2)}) async-start(), calls=%async_computation.29 | async-start | bytes 1769472 | tf_op jit(solution)/shard_map/reduce_scatter | solution.py:68
  717.0 489.7 %reduce-scatter.41.cloned.1.call-start = ((), (), s32[]{:S(2)}) async-start(), calls=%async_computation.28 | async-start | bytes 1769472 | tf_op jit(solution)/shard_map/reduce_scatter | solution.py:68
  747.8 496.4 %reduce-scatter.39.cloned.1.call-start = ((), (), s32[]{:S(2)}) async-start(), calls=%async_computation.27 | async-start | bytes 3440640 | tf_op jit(solution)/shard_map/reduce_scatter | solution.py:62
  754.0 621.5 %all-reduce.4.cloned.1.call-start = ((), (), s32[]{:S(2)}) async-start(), calls=%async_computation.36 | async-start | bytes 196608 | tf_op jit(solution)/shard_map/psum | solution.py:272
  (114 other events, 3976.1 us)
Sparse Core Ops, SparseCore 0:
  11.8 27.4 all-gather.4
  68.4 35.4 reduce-scatter.24
  106.9 26.2 all-gather.6
  159.8 35.4 reduce-scatter.26
  198.3 26.2 all-gather.8
  253.3 35.4 reduce-scatter.28
  291.8 38.8 all-gather.10
  380.7 35.4 reduce-scatter.32
  497.8 35.4 reduce-scatter.34
  535.9 35.4 reduce-scatter.30
  624.4 35.4 reduce-scatter.36
  663.7 66.9 reduce-scatter.54
  735.0 61.5 reduce-scatter.50
  799.9 65.9 reduce-scatter.52
  869.3 66.6 reduce-scatter.46
  939.4 66.6 reduce-scatter.44
  1009.3 61.5 reduce-scatter.48
  1074.6 64.1 reduce-scatter.42
  1142.2 64.3 reduce-scatter.40
  1209.2 34.8 reduce-scatter.38
  1251.5 123.9 all-reduce.3
